TPU v7x, 32 devices: a whole 2x2x4 slice. The times are simulated.
32 devices in a mesh: rep: 8 (over y, x, core), shard: 4 (over z).
Axes of the slice: x: 2, y: 2, z: 4, core: 2. Of those that a mesh axis runs over, the one named last changes fastest.
Arguments:
- tokens: bfloat16 [16, 1024, 768], P('rep', 'shard'), may hold values from -6 to 6
- gain_attn: bfloat16 [768], P('shard'), may hold values from 0.25 to 1.75
- bias_attn: bfloat16 [768], P('shard'), may hold values from -1.5 to 1.5
- w_qkv: bfloat16 [768, 2304], P('shard'), may hold values from -0.21875 to 0.21875
- w_feature: bfloat16 [768, 128], P('shard'), may hold values from -1.5 to 1.5
- w_out: bfloat16 [768, 768], P('shard'), may hold values from -0.875 to 0.875
- gain_mlp: bfloat16 [768], P('shard'), may hold values from 0.25 to 1.75
- bias_mlp: bfloat16 [768], P('shard'), may hold values from -1.5 to 1.5
- w_up: bfloat16 [768, 3072], P('shard'), may hold values from -0.21875 to 0.21875
- w_down: bfloat16 [3072, 768], P('shard'), may hold values from -0.109375 to 0.109375
- cotangent: bfloat16 [16, 1024, 768], P('rep', 'shard'), may hold values from -6 to 6
Outputs:
- block_out: bfloat16 [16, 1024, 768], P('rep', 'shard')
- grad_tokens: bfloat16 [16, 1024, 768], P('rep', 'shard')
- grad_gain_attn: float32 [768], P('shard')
- grad_bias_attn: float32 [768], P('shard')
- grad_w_qkv: float32 [768, 2304], P('shard')
- grad_w_feature: float32 [768, 128], P('shard')
- grad_w_out: float32 [768, 768], P('shard')
- grad_gain_mlp: float32 [768], P('shard')
- grad_bias_mlp: float32 [768], P('shard')
- grad_w_up: float32 [768, 3072], P('shard')
- grad_w_down: float32 [3072, 768], P('shard')
All inputs are finite; a program needn't handle non-finite values.
Results may differ from a plain program's by a relative error of at most 0.019.
Values may be sent and summed in bfloat16 or wider, within the bound.
No kernel may reach another device: no remote copies, remote signals or barrier semaphores. Data moves between devices by JAX's collectives and lax.ppermute only.
A program may use at most 192 MiB of HBM per device.

v0:
```python
import jax
import jax.numpy as jnp
from jax import lax
from jax.sharding import PartitionSpec as P

D = 768
HEADS = 12
HEAD = 64
FEAT = 128
STRETCH = 64
top_precision = lax.Precision.HIGHEST
norm_epsilon = 1e-05


def prefix(value, axis, combine, identity):
    count, here = (lax.axis_size(axis), lax.axis_index(axis))
    everything = jax.tree.map(
        lambda part, kind: lax.all_gather(part.astype(kind), axis),
        value,
        (jnp.bfloat16, jnp.bfloat16),
    )
    start = jax.tree.map(
        lambda part, zero: jnp.broadcast_to(jnp.asarray(zero, part.dtype), part.shape),
        value,
        identity,
    )

    def lap(k, before):
        reached = k < here
        new = combine(
            before, jax.tree.map(lambda part, own: part[k].astype(own.dtype), everything, value)
        )
        return jax.tree.map(lambda a, b: jnp.where(reached, a, b), new, before)

    return lax.fori_loop(0, count, lap, start)


def prefix_2(value, axis, join, neutral):
    count = lax.axis_size(axis)
    place = lax.axis_index(axis)
    ahead = count - 1 - place
    gathered = jax.tree.map(
        lambda a, kind: lax.all_gather(a.astype(kind), axis),
        value,
        jax.tree.map(lambda a: jnp.bfloat16 if a.dtype == jnp.float32 else a.dtype, value),
    )
    state = jax.tree.map(lambda a, e: jnp.zeros_like(a) + jnp.asarray(e, a.dtype), value, neutral)

    def one(lap, state):
        source = count - 1 - lap
        return join(
            state,
            jax.tree.map(
                lambda a, own: lax.dynamic_index_in_dim(a, source, 0, False).astype(own.dtype),
                gathered,
                value,
            ),
        )

    return lax.fori_loop(0, ahead, one, state)


def layer_norm(rows_in, gain, offset):
    centred = rows_in - jnp.mean(rows_in, axis=-1, keepdims=True)
    spread = jnp.mean(centred * centred, axis=-1, keepdims=True)
    return centred * lax.rsqrt(spread + norm_epsilon) * gain + offset


def featurize(inputs):
    return jnp.concatenate(
        [jax.nn.softmax(inputs, axis=-1), jax.nn.softmax(-inputs, axis=-1)], axis=-1
    )


def featurize_pair(u_query, u_key):
    return (featurize(u_query), featurize(u_key))


def gelu_tanh(pre_act):
    return jax.nn.gelu(pre_act, approximate=True)


def add_states(earlier, later):
    return jax.tree.map(jnp.add, earlier, later)


def shifted_sum(terms):
    running = jnp.cumsum(terms, axis=0)
    return jnp.concatenate([jnp.zeros_like(terms[:1]), running[:-1]], axis=0)


def attend_local(query_wide, key_wide, value_wide, prior_state, prior_total):
    length = query_wide.shape[0]
    blocks = length // STRETCH
    block_q = query_wide.reshape(blocks, STRETCH, HEADS, FEAT)
    block_k = key_wide.reshape(blocks, STRETCH, HEADS, FEAT)
    block_v = value_wide.reshape(blocks, STRETCH, HEADS, HEAD)
    state_terms = jnp.einsum("nshf,nshe->nhfe", block_k, block_v, precision=top_precision)
    total_terms = jnp.sum(block_k, axis=1)
    state_before = prior_state[None] + shifted_sum(state_terms)
    total_before = prior_total[None] + shifted_sum(total_terms)
    positions = jnp.arange(STRETCH)
    causal = positions[:, None] >= positions[None, :]
    scores = jnp.where(
        causal, jnp.einsum("nthf,nshf->nhts", block_q, block_k, precision=top_precision), 0.0
    )
    numerator = jnp.einsum("nhts,nshe->nthe", scores, block_v, precision=top_precision)
    numerator = numerator + jnp.einsum(
        "nthf,nhfe->nthe", block_q, state_before, precision=top_precision
    )
    denominator = jnp.transpose(jnp.sum(scores, axis=3), (0, 2, 1))
    denominator = denominator + jnp.einsum(
        "nthf,nhf->nth", block_q, total_before, precision=top_precision
    )
    return (numerator / denominator[..., None]).reshape(length, HEADS, HEAD)


def shards(
    tokens,
    gain_attn,
    bias_attn,
    w_qkv,
    w_feature,
    w_out,
    gain_mlp,
    bias_mlp,
    w_up,
    w_down,
    cotangent,
):
    shard_count = lax.axis_size("shard")
    local_weights = (
        gain_attn,
        bias_attn,
        w_qkv,
        w_feature,
        w_out,
        gain_mlp,
        bias_mlp,
        w_up,
        w_down,
    )
    totals = [
        jnp.zeros((weight.shape[0] * shard_count,) + weight.shape[1:], jnp.float32)
        for weight in local_weights
    ]
    results = []
    input_grads = []
    for batch_index in range(tokens.shape[0]):
        forward_set = (
            lax.all_gather(gain_attn, "shard", axis=0, tiled=True),
            lax.all_gather(bias_attn, "shard", axis=0, tiled=True),
            lax.all_gather(w_qkv, "shard", axis=0, tiled=True),
            lax.all_gather(w_feature, "shard", axis=0, tiled=True),
            lax.all_gather(w_out, "shard", axis=0, tiled=True),
            lax.all_gather(gain_mlp, "shard", axis=0, tiled=True),
            lax.all_gather(bias_mlp, "shard", axis=0, tiled=True),
            lax.all_gather(w_up, "shard", axis=0, tiled=True),
            lax.all_gather(w_down, "shard", axis=0, tiled=True),
        )
        (
            gain_one,
            bias_one,
            qkv_weight,
            feature_weight,
            out_weight,
            gain_two,
            bias_two,
            up_weight,
            down_weight,
        ) = forward_set
        rows_in = tokens[batch_index].astype(jnp.float32)
        length = rows_in.shape[0]
        normed, norm_pull = jax.vjp(
            layer_norm, rows_in, gain_one.astype(jnp.float32), bias_one.astype(jnp.float32)
        )
        normed_low = normed.astype(jnp.bfloat16)
        mixed = jnp.dot(normed_low, qkv_weight, preferred_element_type=jnp.float32).astype(
            jnp.bfloat16
        )
        queries = mixed[:, :D].reshape(length, HEADS, HEAD)
        key_rows = mixed[:, D : 2 * D].reshape(length, HEADS, HEAD)
        values = mixed[:, 2 * D :].reshape(length, HEADS, HEAD)
        feature_maps = feature_weight.reshape(HEADS, HEAD, 2, HEAD)
        u_query = jnp.einsum(
            "thi,hio->tho", queries, feature_maps[:, :, 0], preferred_element_type=jnp.float32
        )
        u_key = jnp.einsum(
            "thi,hio->tho", key_rows, feature_maps[:, :, 1], preferred_element_type=jnp.float32
        )
        (f_query, f_key), feature_pull = jax.vjp(featurize_pair, u_query, u_key)
        query_low = f_query.astype(jnp.bfloat16)
        key_low = f_key.astype(jnp.bfloat16)
        query_wide = query_low.astype(jnp.float32)
        key_wide = key_low.astype(jnp.float32)
        value_wide = values.astype(jnp.float32)
        key_state = jnp.einsum("shf,she->hfe", key_low, values, preferred_element_type=jnp.float32)
        key_sum = jnp.sum(key_wide, axis=0)
        prior = prefix(
            (key_state, key_sum),
            "shard",
            add_states,
            (jnp.zeros_like(key_state), jnp.zeros_like(key_sum)),
        )
        attended, attend_pull = jax.vjp(
            attend_local, query_wide, key_wide, value_wide, prior[0], prior[1]
        )
        attended_low = attended.reshape(length, D).astype(jnp.bfloat16)
        resid = rows_in + jnp.dot(attended_low, out_weight, preferred_element_type=jnp.float32)
        normed_two, norm_two_pull = jax.vjp(
            layer_norm, resid, gain_two.astype(jnp.float32), bias_two.astype(jnp.float32)
        )
        normed_two_low = normed_two.astype(jnp.bfloat16)
        pre_act = jnp.dot(normed_two_low, up_weight, preferred_element_type=jnp.float32)
        hidden, gelu_pull = jax.vjp(gelu_tanh, pre_act)
        hidden_low = hidden.astype(jnp.bfloat16)
        result = resid + jnp.dot(hidden_low, down_weight, preferred_element_type=jnp.float32)
        results.append(result.astype(jnp.bfloat16))
        qkv_back, feature_back, out_back, up_back, down_back = (
            lax.all_gather(w_qkv, "shard", axis=0, tiled=True),
            lax.all_gather(w_feature, "shard", axis=0, tiled=True),
            lax.all_gather(w_out, "shard", axis=0, tiled=True),
            lax.all_gather(w_up, "shard", axis=0, tiled=True),
            lax.all_gather(w_down, "shard", axis=0, tiled=True),
        )
        grad_out = cotangent[batch_index]
        d_down = jnp.dot(hidden_low.T, grad_out, preferred_element_type=jnp.float32)
        d_hidden = jnp.dot(grad_out, down_back.T, preferred_element_type=jnp.float32)
        (d_pre,) = gelu_pull(d_hidden)
        d_pre_low = d_pre.astype(jnp.bfloat16)
        d_up = jnp.dot(normed_two_low.T, d_pre_low, preferred_element_type=jnp.float32)
        d_normed_two = jnp.dot(d_pre_low, up_back.T, preferred_element_type=jnp.float32)
        d_resid_two, d_gain_two, d_bias_two = norm_two_pull(d_normed_two)
        d_resid = grad_out.astype(jnp.float32) + d_resid_two
        d_resid_low = d_resid.astype(jnp.bfloat16)
        d_out = jnp.dot(attended_low.T, d_resid_low, preferred_element_type=jnp.float32)
        d_attended = jnp.dot(d_resid_low, out_back.T, preferred_element_type=jnp.float32).reshape(
            length, HEADS, HEAD
        )
        d_query_f, d_key_f, d_value_f, local_state, local_sum = attend_pull(d_attended)
        later = prefix_2(
            (local_state, local_sum),
            "shard",
            add_states,
            (jnp.zeros_like(local_state), jnp.zeros_like(local_sum)),
        )
        d_key_f = (
            d_key_f
            + jnp.einsum("hfe,she->shf", later[0], value_wide, precision=top_precision)
            + later[1][None]
        )
        d_value_f = d_value_f + jnp.einsum(
            "hfe,shf->she", later[0], key_wide, precision=top_precision
        )
        d_u_query, d_u_key = feature_pull((d_query_f, d_key_f))
        d_uq_low = d_u_query.astype(jnp.bfloat16)
        d_uk_low = d_u_key.astype(jnp.bfloat16)
        back_maps = feature_back.reshape(HEADS, HEAD, 2, HEAD)
        d_queries = jnp.einsum(
            "tho,hio->thi", d_uq_low, back_maps[:, :, 0], preferred_element_type=jnp.float32
        )
        d_keys = jnp.einsum(
            "tho,hio->thi", d_uk_low, back_maps[:, :, 1], preferred_element_type=jnp.float32
        )
        query_map_grad = jnp.einsum(
            "thi,tho->hio", queries, d_uq_low, preferred_element_type=jnp.float32
        )
        key_map_grad = jnp.einsum(
            "thi,tho->hio", key_rows, d_uk_low, preferred_element_type=jnp.float32
        )
        d_maps = jnp.stack([query_map_grad, key_map_grad], axis=2).reshape(D, FEAT)
        d_mixed = jnp.concatenate(
            [d_queries.reshape(length, D), d_keys.reshape(length, D), d_value_f.reshape(length, D)],
            axis=1,
        ).astype(jnp.bfloat16)
        d_qkv = jnp.dot(normed_low.T, d_mixed, preferred_element_type=jnp.float32)
        d_normed = jnp.dot(d_mixed, qkv_back.T, preferred_element_type=jnp.float32)
        d_rows, d_gain_one, d_bias_one = norm_pull(d_normed)
        input_grads.append((d_resid + d_rows).astype(jnp.bfloat16))
        contributions = (
            d_gain_one,
            d_bias_one,
            d_qkv,
            d_maps,
            d_out,
            d_gain_two,
            d_bias_two,
            d_up,
            d_down,
        )
        totals = [total_sum + new_term for total_sum, new_term in zip(totals, contributions)]
    shares = (
        lax.psum_scatter(
            totals[0].astype(jnp.bfloat16), "shard", scatter_dimension=0, tiled=True
        ).astype(jnp.float32),
        lax.psum_scatter(
            totals[1].astype(jnp.bfloat16), "shard", scatter_dimension=0, tiled=True
        ).astype(jnp.float32),
        lax.psum_scatter(
            totals[2].astype(jnp.bfloat16), "shard", scatter_dimension=0, tiled=True
        ).astype(jnp.float32),
        lax.psum_scatter(
            totals[3].astype(jnp.bfloat16), "shard", scatter_dimension=0, tiled=True
        ).astype(jnp.float32),
        lax.psum_scatter(
            totals[4].astype(jnp.bfloat16), "shard", scatter_dimension=0, tiled=True
        ).astype(jnp.float32),
        lax.psum_scatter(
            totals[5].astype(jnp.bfloat16), "shard", scatter_dimension=0, tiled=True
        ).astype(jnp.float32),
        lax.psum_scatter(
            totals[6].astype(jnp.bfloat16), "shard", scatter_dimension=0, tiled=True
        ).astype(jnp.float32),
        lax.psum_scatter(
            totals[7].astype(jnp.bfloat16), "shard", scatter_dimension=0, tiled=True
        ).astype(jnp.float32),
        lax.psum_scatter(
            totals[8].astype(jnp.bfloat16), "shard", scatter_dimension=0, tiled=True
        ).astype(jnp.float32),
    )
    reduced = (
        lax.psum(shares[0].astype(jnp.bfloat16), "rep").astype(jnp.float32),
        lax.psum(shares[1].astype(jnp.bfloat16), "rep").astype(jnp.float32),
        lax.psum(shares[2].astype(jnp.bfloat16), "rep").astype(jnp.float32),
        lax.psum(shares[3].astype(jnp.bfloat16), "rep").astype(jnp.float32),
        lax.psum(shares[4].astype(jnp.bfloat16), "rep").astype(jnp.float32),
        lax.psum(shares[5].astype(jnp.bfloat16), "rep").astype(jnp.float32),
        lax.psum(shares[6].astype(jnp.bfloat16), "rep").astype(jnp.float32),
        lax.psum(shares[7].astype(jnp.bfloat16), "rep").astype(jnp.float32),
        lax.psum(shares[8].astype(jnp.bfloat16), "rep").astype(jnp.float32),
    )
    return (
        jnp.stack(results),
        jnp.stack(input_grads),
        reduced[0],
        reduced[1],
        reduced[2],
        reduced[3],
        reduced[4],
        reduced[5],
        reduced[6],
        reduced[7],
        reduced[8],
    )


def solution(mesh):
    placed = (
        P("rep", "shard", None),
        P("shard"),
        P("shard"),
        P("shard", None),
        P("shard", None),
        P("shard", None),
        P("shard"),
        P("shard"),
        P("shard", None),
        P("shard", None),
        P("rep", "shard", None),
    )
    return jax.shard_map(
        shards,
        mesh=mesh,
        in_specs=placed,
        out_specs=(
            P("rep", "shard", None),
            P("rep", "shard", None),
            P("shard"),
            P("shard"),
            P("shard", None),
            P("shard", None),
            P("shard", None),
            P("shard"),
            P("shard"),
            P("shard", None),
            P("shard", None),
        ),
        check_vma=False,
    )
```

profile of v0, /device:TPU:0, one launch (start us, length us, event | category | flops | bytes accessed | tf_op | source)
XLA Modules:
  0.0 919.0 jit_solution(16887876758495918346)
XLA Ops:
  14.7 14.5 %all-reduce.15 = (bf16[768]{0:T(1024)(128)(2,1)S(1)}, bf16[768]{0:T(1024)(128)(2,1)S(1)}, bf16[768]{0:T(1024)(128)(2,1)}, bf16[768]{0:T(1024)(128)(2,1)}) all-reduce(bf16[768]{0:T(1024)(128)(2,1)S(1)} %dynamic-update-slice.1, bf16[768]{0:T(1024)(128)(2,1)S(1)} %dynamic-update-slice, ...), channel_id=1, replica_groups=mesh['rep'=8,'shard'=4] {'shard'}, use_global_device_ids=true, to_apply=%add.5 | all-reduce | flops 3072 | bytes 12288
  30.4 14.9 %all_gather.89 = bf16[768,128]{1,0:T(8,128)(2,1)S(1)} all-gather(bf16[192,128]{1,0:T(8,128)(2,1)S(1)} %copy-done.179), channel_id=1, replica_groups=mesh['rep'=8,'shard'=4] {'shard'}, dimensions={0}, use_global_device_ids=true | all-gather | bytes 245760 | tf_op jit(solution)/shard_map/all_gather | solution.py:154
  51.4 34.1 %all-gather.17.cloned.1.call-done = bf16[768,2304]{1,0:T(8,128)(2,1)} async-done(((bf16[192,2304]{1,0:T(8,128)(2,1)}), bf16[768,2304]{1,0:T(8,128)(2,1)}) %all-gather.17.cloned.1.call-update) | async-done | bytes 3538960 | tf_op jit(solution)/shard_map/all_gather | solution.py:153
  85.5 3.2 convolution_convert_fusion
  110.0 3.2 convolution_convert_fusion.1
  159.9 30.2 %all-gather.2 = bf16[48,128,64]{1,2,0:T(8,128)(2,1)} all-gather(bf16[12,128,64]{1,2,0:T(8,128)(2,1)S(1)} %convolution_convert_fusion.6), channel_id=4, replica_groups=mesh['rep'=8,'shard'=4] {'shard'}, dimensions={0}, use_global_device_ids=true | all-gather | bytes 983040 | tf_op jit(solution)/shard_map/all_gather | solution.py:18
  190.1 13.3 %all-gather.9 = bf16[4,12,128]{2,1,0:T(8,128)(2,1)S(1)} all-gather(bf16[1,12,128]{2,1,0:T(8,128)(2,1)S(1)} %bitcast.581), channel_id=5, replica_groups=mesh['rep'=8,'shard'=4] {'shard'}, dimensions={0}, use_global_device_ids=true | all-gather | bytes 15360 | tf_op jit(solution)/shard_map/all_gather | solution.py:18
  203.4 6.6 while.63
  226.2 4.9 fusion.40
  249.9 30.3 %all-gather = bf16[48,128,64]{1,2,0:T(8,128)(2,1)} all-gather(bf16[12,128,64]{1,2,0:T(8,128)(2,1)S(1)} %convolution_convert_fusion.7), channel_id=2, replica_groups=mesh['rep'=8,'shard'=4] {'shard'}, dimensions={0}, use_global_device_ids=true | all-gather | bytes 983040 | tf_op jit(solution)/shard_map/all_gather | solution.py:18
  280.2 13.9 %all-gather.8 = bf16[4,12,128]{2,1,0:T(8,128)(2,1)S(1)} all-gather(bf16[1,12,128]{2,1,0:T(8,128)(2,1)S(1)} %bitcast.580), channel_id=3, replica_groups=mesh['rep'=8,'shard'=4] {'shard'}, dimensions={0}, use_global_device_ids=true | all-gather | bytes 15360 | tf_op jit(solution)/shard_map/all_gather | solution.py:18
  294.1 6.6 while.62
  332.0 5.6 fusion.215
  337.6 3.2 fusion.214
  340.8 6.4 fusion.21
  348.4 3.9 fusion.265
  365.0 4.5 fusion.255
  371.3 3.9 fusion.29
  376.6 3.1 reshape_reshape.6
  379.8 4.5 fusion.254
  387.3 3.9 fusion.38
  396.4 3.8 add_bitcast_fusion
  400.3 19.6 %all-gather.6 = bf16[48,128,64]{1,2,0:T(8,128)(2,1)} all-gather(bf16[12,128,64]{1,2,0:T(8,128)(2,1)S(1)} %copy-done.148), channel_id=8, replica_groups=mesh['rep'=8,'shard'=4] {'shard'}, dimensions={0}, use_global_device_ids=true | all-gather | bytes 983040 | tf_op jit(solution)/shard_map/all_gather | solution.py:43
  419.9 13.1 %all-gather.11 = bf16[4,12,128]{2,1,0:T(8,128)(2,1)S(1)} all-gather(bf16[1,12,128]{2,1,0:T(8,128)(2,1)S(1)} %bitcast.583), channel_id=9, replica_groups=mesh['rep'=8,'shard'=4] {'shard'}, dimensions={0}, use_global_device_ids=true | all-gather | bytes 15360 | tf_op jit(solution)/shard_map/all_gather | solution.py:43
  433.1 4.7 while.61
  445.1 3.2 copy.227
  470.6 3.8 add_bitcast_fusion.2
  474.4 16.5 %all-gather.4 = bf16[48,128,64]{1,2,0:T(8,128)(2,1)} all-gather(bf16[12,128,64]{1,2,0:T(8,128)(2,1)S(1)} %copy-done.147), channel_id=6, replica_groups=mesh['rep'=8,'shard'=4] {'shard'}, dimensions={0}, use_global_device_ids=true | all-gather | bytes 983040 | tf_op jit(solution)/shard_map/all_gather | solution.py:43
  490.9 13.1 %all-gather.10 = bf16[4,12,128]{2,1,0:T(8,128)(2,1)S(1)} all-gather(bf16[1,12,128]{2,1,0:T(8,128)(2,1)S(1)} %bitcast.582), channel_id=7, replica_groups=mesh['rep'=8,'shard'=4] {'shard'}, dimensions={0}, use_global_device_ids=true | all-gather | bytes 15360 | tf_op jit(solution)/shard_map/all_gather | solution.py:43
  504.1 4.3 while.60
  515.8 3.1 copy.205
  533.6 3.2 add_convert_fusion.3
  537.1 3.1 add_convert_fusion.8
  547.5 3.6 copy.208
  563.2 3.2 add_convert_fusion.2
  567.5 3.3 fusion.213
  570.8 3.8 add_convert_fusion.1
  575.8 4.3 fusion.129
  580.1 3.9 add_convert_fusion
  591.5 3.5 fusion.119
  599.4 5.2 fusion.78
  604.8 24.6 %reduce-scatter.6.cloned.1.call-done = bf16[192,2304]{1,0:T(8,128)(2,1)} async-done(((bf16[768,2304]{1,0:T(8,128)(2,1)}), bf16[192,2304]{1,0:T(8,128)(2,1)}) %reduce-scatter.6.cloned.1.call-update) | async-done | bytes 884752 | tf_op jit(solution)/shard_map/reduce_scatter | solution.py:299
  629.4 87.9 %reduce-scatter.12.cloned.1.call-done = bf16[192,3072]{1,0:T(8,128)(2,1)} async-done(((bf16[768,3072]{1,0:T(8,128)(2,1)}), bf16[192,3072]{1,0:T(8,128)(2,1)}) %reduce-scatter.12.cloned.1.call-update) | async-done | bytes 1179664 | tf_op jit(solution)/shard_map/reduce_scatter | solution.py:314
  717.2 88.1 %reduce-scatter.14.cloned.1.call-done = bf16[768,768]{1,0:T(8,128)(2,1)} async-done(((bf16[3072,768]{1,0:T(8,128)(2,1)}), bf16[768,768]{1,0:T(8,128)(2,1)}) %reduce-scatter.14.cloned.1.call-update) | async-done | bytes 1179664 | tf_op jit(solution)/shard_map/reduce_scatter | solution.py:317
  806.0 11.1 %all-reduce.14 = (bf16[768]{0:T(1024)(128)(2,1)S(1)}, bf16[768]{0:T(1024)(128)(2,1)S(1)}, bf16[768]{0:T(1024)(128)(2,1)S(1)}, bf16[768]{0:T(1024)(128)(2,1)S(1)}) all-reduce(bf16[768]{0:T(1024)(128)(2,1)S(1)} %copy-done.224, bf16[768]{0:T(1024)(128)(2,1)S(1)} %add_convert_fusion.14, ...), channel_id=10, replica_groups=mesh['rep'=8,'shard'=4] {'shard'}, use_global_device_ids=true, to_apply=%region_70.71.clone | all-reduce | flops 3072 | bytes 12288
  817.4 5.4 fusion.79
  828.2 24.5 %all-reduce.12 = (bf16[192]{0:T(256)(128)(2,1)S(1)}, bf16[192]{0:T(256)(128)(2,1)S(1)}, bf16[192,128]{1,0:T(8,128)(2,1)S(1)}, bf16[192]{0:T(256)(128)(2,1)S(1)}, bf16[192]{0:T(256)(128)(2,1)S(1)}) all-reduce(bf16[192]{0:T(256)(128)(2,1)S(1)} %dynamic-slice.5, ...), channel_id=1, replica_groups=mesh['rep'=8,'shard'=4] {'rep'}, use_global_device_ids=true, to_apply=%region_71.72 | all-reduce | flops 25344 | bytes 101376 | tf_op jit(solution)/shard_map/psum | solution.py:322
  855.6 49.7 %all-reduce.18.cloned.1.call-done = (bf16[192,2304]{1,0:T(8,128)(2,1)}, bf16[192,768]{1,0:T(8,128)(2,1)}, bf16[192,3072]{1,0:T(8,128)(2,1)}, bf16[768,768]{1,0:T(8,128)(2,1)}) async-done(((bf16[192,2304]{1,0:T(8,128)(2,1)}, bf16[192,768]{1,0:T(8,128)(2,1)}, bf16[192,3072]{1,0:T(8,128)(2,1)}, bf16[768,768]{1,0:T(8,128)(2,1)}), (bf16[192,2304]{1,0:T(8,128)(2,1)}, bf16[192,768]{1,0:T(8,128)(2,1)}, ...) | async-done | bytes 3538960 | tf_op jit(solution)/shard_map/psum | solution.py:324
  (804 shorter events, 293.3 us)
Async XLA Ops:
  7.2 78.3 %all-gather.17.cloned.1.call-start = ((), (), s32[]{:S(2)}) async-start(), calls=%async_computation.5 | async-start | bytes 4423680 | tf_op jit(solution)/shard_map/all_gather | solution.py:153
  7.9 313.2 %all-gather.19.cloned.1.call-start = ((), (), s32[]{:S(2)}) async-start(), calls=%async_computation.6 | async-start | bytes 1474560 | tf_op jit(solution)/shard_map/all_gather | solution.py:155
  8.7 323.3 %all-gather.21.cloned.1.call-start = ((), (), s32[]{:S(2)}) async-start(), calls=%async_computation.7 | async-start | bytes 5898240 | tf_op jit(solution)/shard_map/all_gather | solution.py:158
  9.5 20.9 %copy-start.179 = (bf16[192,128]{1,0:T(8,128)(2,1)S(1)}, bf16[192,128]{1,0:T(8,128)(2,1)}, u32[]{:S(2)}) copy-start(bf16[192,128]{1,0:T(8,128)(2,1)} %param.23) | copy-start | bytes 147460
  9.5 331.4 %all-gather.23.cloned.1.call-start = ((), (), s32[]{:S(2)}) async-start(), calls=%async_computation.8 | async-start | bytes 5898240 | tf_op jit(solution)/shard_map/all_gather | solution.py:159
  10.0 594.7 %reduce-scatter.10.cloned.1.call-start = ((), (), s32[]{:S(2)}) async-start(), calls=%async_computation.11 | async-start | bytes 1474560 | tf_op jit(solution)/shard_map/reduce_scatter | solution.py:305
  10.9 34.4 %copy-start.180 = (f32[256]{0:T(256)}, f32[256]{0:T(256)S(1)}, u32[]{:S(2)}) copy-start(f32[256]{0:T(256)S(1)} %get-tuple-element.658) | copy-start | bytes 3076
  10.9 34.4 %copy-start.188 = (f32[256]{0:T(256)}, f32[256]{0:T(256)S(1)}, u32[]{:S(2)}) copy-start(f32[256]{0:T(256)S(1)} %get-tuple-element.657) | copy-start | bytes 3076
  11.8 33.5 %copy-start.215 = (f32[256]{0:T(256)}, f32[256]{0:T(256)S(1)}, u32[]{:S(2)}) copy-start(f32[256]{0:T(256)S(1)} %get-tuple-element.512) | copy-start | bytes 3076
  47.2 45.6 %copy-start.72 = (bf16[12,64,1,64]{1,3,0,2:T(8,128)(2,1)}, bf16[12,64,1,64]{1,3,0,2:T(8,128)(2,1)S(1)}, u32[]{:S(2)}) copy-start(bf16[12,64,1,64]{1,3,0,2:T(8,128)(2,1)S(1)} %copy.272) | copy-start | bytes 294916
  47.5 51.9 %copy-start.75 = (bf16[12,64,1,64]{1,3,0,2:T(8,128)(2,1)}, bf16[12,64,1,64]{1,3,0,2:T(8,128)(2,1)S(1)}, u32[]{:S(2)}) copy-start(bf16[12,64,1,64]{1,3,0,2:T(8,128)(2,1)S(1)} %copy.273) | copy-start | bytes 294916
  91.0 5.6 copy-start.93
  102.9 56.7 %copy-start.63 = (bf16[256,12,64]{0,2,1:T(8,128)(2,1)}, bf16[256,12,64]{0,2,1:T(8,128)(2,1)S(1)}, u32[]{:S(2)}) copy-start(bf16[256,12,64]{0,2,1:T(8,128)(2,1)S(1)} %divide_convert_fusion) | copy-start | bytes 1179652
  115.5 5.7 copy-start.96
  115.5 5.6 copy-start.76
  126.1 6.4 copy-start.15
  158.3 31.8 %copy-start.83 = (bf16[256,768]{0,1:T(8,128)(2,1)}, bf16[256,768]{0,1:T(8,128)(2,1)S(1)}, u32[]{:S(2)}) copy-start(bf16[256,768]{0,1:T(8,128)(2,1)S(1)} %copy.174) | copy-start | bytes 1179652
  159.5 30.6 %copy-start.199 = (bf16[12,128]{1,0:T(8,128)(2,1)S(1)}, bf16[12,128]{1,0:T(8,128)(2,1)}, u32[]{:S(2)}) copy-start(bf16[12,128]{1,0:T(8,128)(2,1)} %fusion.139) | copy-start | bytes 9220
  224.2 6.9 copy-start.132
  248.2 32.0 %copy-start.81 = (bf16[256,768]{0,1:T(8,128)(2,1)}, bf16[256,768]{0,1:T(8,128)(2,1)S(1)}, u32[]{:S(2)}) copy-start(bf16[256,768]{0,1:T(8,128)(2,1)S(1)} %copy.157) | copy-start | bytes 1179652
  249.5 30.7 %copy-start.198 = (bf16[12,128]{1,0:T(8,128)(2,1)S(1)}, bf16[12,128]{1,0:T(8,128)(2,1)}, u32[]{:S(2)}) copy-start(bf16[12,128]{1,0:T(8,128)(2,1)} %fusion.140) | copy-start | bytes 9220
  302.6 11.5 %copy-start.2 = (bf16[4,64,12,128]{3,1,2,0:T(8,128)(2,1)}, bf16[4,64,12,128]{3,1,2,0:T(8,128)(2,1)S(1)}, u32[]{:S(2)}) copy-start(bf16[4,64,12,128]{3,1,2,0:T(8,128)(2,1)S(1)} %get-tuple-element.589) | copy-start | bytes 2359300
  310.1 6.4 copy-start.134
  323.3 34.7 %copy-start.11 = (f32[256,768]{1,0:T(8,128)}, f32[256,768]{1,0:T(8,128)S(1)}, u32[]{:S(2)}) copy-start(f32[256,768]{1,0:T(8,128)S(1)} %get-tuple-element.636) | copy-start | bytes 2359300
  324.2 5.3 copy-start.151
  324.2 5.9 copy-start.138
  324.2 6.5 copy-start.137
  324.2 7.1 copy-start.150
  324.8 5.9 copy-start.191
  325.9 5.4 copy-start.220
  331.9 5.6 copy-start.26
  331.9 5.6 copy-start.144
  332.0 5.6 copy-start.156
  332.0 5.6 copy-start.192
  332.0 5.6 copy-start.204
  332.0 5.6 copy-start.235
  340.8 11.4 %copy-start.234 = (bf16[3072,768]{1,0:T(8,128)(2,1)S(1)}, bf16[3072,768]{1,0:T(8,128)(2,1)}, u32[]{:S(2)}) copy-start(bf16[3072,768]{1,0:T(8,128)(2,1)} %all-gather.23.cloned.1.call-done) | copy-start | bytes 14155780
  348.4 7.0 slice-start.2
  470.6 20.4 %copy-start.200 = (bf16[12,128]{1,0:T(8,128)(2,1)S(1)}, bf16[12,128]{1,0:T(8,128)(2,1)}, u32[]{:S(2)}) copy-start(bf16[12,128]{1,0:T(8,128)(2,1)} %fusion.187) | copy-start | bytes 9220
  536.8 92.5 %reduce-scatter.6.cloned.1.call-start = ((), (), s32[]{:S(2)}) async-start(), calls=%async_computation.9 | async-start | bytes 4423680 | tf_op jit(solution)/shard_map/reduce_scatter | solution.py:299
  566.5 150.8 %reduce-scatter.12.cloned.1.call-start = ((), (), s32[]{:S(2)}) async-start(), calls=%async_computation.12 | async-start | bytes 5898240 | tf_op jit(solution)/shard_map/reduce_scatter | solution.py:314
  574.7 230.6 %reduce-scatter.14.cloned.1.call-start = ((), (), s32[]{:S(2)}) async-start(), calls=%async_computation.13 | async-start | bytes 5898240 | tf_op jit(solution)/shard_map/reduce_scatter | solution.py:317
  584.0 244.1 %reduce-scatter.8.cloned.1.call-start = ((), (), s32[]{:S(2)}) async-start(), calls=%async_computation.10 | async-start | bytes 245760 | tf_op jit(solution)/shard_map/reduce_scatter | solution.py:302
  599.2 306.1 %all-reduce.18.cloned.1.call-start = ((), (), s32[]{:S(2)}) async-start(), calls=%async_computation.14 | async-start | bytes 7077888 | tf_op jit(solution)/shard_map/psum | solution.py:324
  817.4 6.4 copy-start.226
  817.4 6.4 copy-start.225
  817.4 6.4 copy-start.103
  817.4 6.4 copy-start.105
  (207 other events, 536.4 us)
Sparse Core Ops, SparseCore 0:
  9.6 75.8 all-gather.16
  87.1 29.1 all-gather.18
  117.9 101.2 all-gather.20
  220.5 100.6 all-gather.22
  536.9 25.0 reduce-scatter.9
  566.5 62.7 reduce-scatter.5
  631.7 85.5 reduce-scatter.11
  719.5 85.7 reduce-scatter.13
  808.2 19.9 reduce-scatter.7
  832.1 73.0 all-reduce.17
where the time goes:
time: 925 us; the launch traced here: 919 us
  waiting for transfers between devices  289 us (31%)
  blocking collectives  215 us (23%)
  matrix products  169 us (18%)
  local copies, waits for them, and re-layouts  144 us (16%)
  other arithmetic  81.6 us (9%)
  between operations  18.6 us (2%)
    reduce_scatter x1, waiting for transfers between devices, shards(): lax.psum_scatter(totals[8].astype(jnp.bfloat16), 'shard', scatter_dimensi...  88.1 us
    reduce_scatter x1, waiting for transfers between devices, shards(): lax.psum_scatter(totals[7].astype(jnp.bfloat16), 'shard', scatter_dimensi...  87.9 us
    all_gather x4, blocking collectives, prefix(): lax.all_gather(part.astype(kind), axis)  87.6 us
    all_gather x4, blocking collectives, prefix_2(): lax.all_gather(a.astype(kind), axis)  62.3 us
    psum x1, waiting for transfers between devices, shards(): lax.psum(shares[2].astype(jnp.bfloat16), 'rep').astype(jnp.float32)  49.7 us
    all_gather x1, waiting for transfers between devices, shards(): lax.all_gather(w_qkv, 'shard', axis=0, tiled=True)  34.1 us
    unnamed x505, local copies, waits for them, and re-layouts  32.8 us
    concatenate x16, local copies, waits for them, and re-layouts, featurize(): jnp.concatenate([jax.nn.softmax(inputs, axis=-1), jax.nn.softmax(-inputs,...  32.5 us
  transfers between devices with their start and end apart: 10, of which 6 were waited for; matrix products, arithmetic and copies ran while one was open for 27% of the time, Pallas kernels for 0%

commit v1 on v0

--- a/solution.py
+++ b/solution.py
@@ -1,3 +1,4 @@
+import functools
 import jax
 import jax.numpy as jnp
 from jax import lax
@@ -10,6 +11,28 @@
 STRETCH = 64
 top_precision = lax.Precision.HIGHEST
 norm_epsilon = 1e-05
+
+
+def produce_orders(x0, named_axis):
+    then, local_part, mat_out = (
+        jax.lax.axis_size(named_axis),
+        jax.lax.axis_index(named_axis),
+        x0.shape[0],
+    )
+    ledger = []
+    for w in range(then):
+        ledger.append((w, (w + 1) % then))
+    w1 = jnp.zeros((*x0.shape[:0], then * mat_out, *x0.shape[1:]), x0.dtype)
+    upper = x0
+    for to_i in range(then):
+        p_next = (local_part - to_i) % then
+        w1 = lax.dynamic_update_slice_in_dim(w1, upper, p_next * mat_out, axis=0)
+        if to_i < then - 1:
+            upper = jax.lax.ppermute(upper, named_axis, ledger)
+    return w1
+
+
+track_lanes = functools.partial(produce_orders, named_axis="shard")
 
 
 def prefix(value, axis, combine, identity):
@@ -150,7 +173,7 @@
         forward_set = (
             lax.all_gather(gain_attn, "shard", axis=0, tiled=True),
             lax.all_gather(bias_attn, "shard", axis=0, tiled=True),
-            lax.all_gather(w_qkv, "shard", axis=0, tiled=True),
+            track_lanes(w_qkv),
             lax.all_gather(w_feature, "shard", axis=0, tiled=True),
             lax.all_gather(w_out, "shard", axis=0, tiled=True),
             lax.all_gather(gain_mlp, "shard", axis=0, tiled=True),

time: 925 us -> 1020 us (1.10)
  blocking collectives: 215 us -> 275 us
  other arithmetic: 81.6 us -> 92.1 us
    unnamed x2, blocking collectives: 25.6 us -> 69.8 us
    all_gather x1, blocking collectives: 14.9 us -> 53.3 us  [shards(): lax.all_gather(w_feature, 'shard', axis=0, tiled=True)]
    all_gather x1, waiting for transfers between devices: 34.1 us -> 0.01 us  [shards(): lax.all_gather(w_qkv, 'shard', axis=0, tiled=True)]
    ppermute x0 -> x3, waiting for transfers between devices: none -> 31.6 us  [produce_orders(): upper = jax.lax.ppermute(upper, named_axis, ledger)]
    all_gather x4, blocking collectives: 87.6 us -> 67.5 us  [prefix(): lax.all_gather(part.astype(kind), axis)]
    unnamed x505 -> x519, local copies, waits for them, and re-layouts: 32.8 us -> 34 us
  transfers between devices with their start and end apart: 10 -> 13, of which waited for: 6 -> 6; matrix products, arithmetic and copies ran while one was open for 27% -> 39% of each run, Pallas kernels for 0% -> 0%
where the time goes in v1:
time: 1020 us; the launch traced here: 1010 us
  waiting for transfers between devices  291 us (29%)
  blocking collectives  275 us (27%)
  matrix products  178 us (17%)
  local copies, waits for them, and re-layouts  149 us (15%)
  other arithmetic  92.1 us (9%)
  between operations  18.6 us (2%)
  starting transfers between devices  10.4 us (1%)
    reduce_scatter x1, waiting for transfers between devices, shards(): lax.psum_scatter(totals[8].astype(jnp.bfloat16), 'shard', scatter_dimensi...  88.1 us
    reduce_scatter x1, waiting for transfers between devices, shards(): lax.psum_scatter(totals[7].astype(jnp.bfloat16), 'shard', scatter_dimensi...  87.9 us
    unnamed x2, blocking collectives  69.8 us
    all_gather x4, blocking collectives, prefix(): lax.all_gather(part.astype(kind), axis)  67.5 us
    all_gather x4, blocking collectives, prefix_2(): lax.all_gather(a.astype(kind), axis)  59.4 us
    all_gather x1, blocking collectives, shards(): lax.all_gather(w_feature, 'shard', axis=0, tiled=True)  53.3 us
    psum x1, waiting for transfers between devices, shards(): lax.psum(shares[2].astype(jnp.bfloat16), 'rep').astype(jnp.float32)  49.7 us
    unnamed x519, local copies, waits for them, and re-layouts  34 us
  transfers between devices with their start and end apart: 13, of which 6 were waited for; matrix products, arithmetic and copies ran while one was open for 39% of the time, Pallas kernels for 0%

profile of v1, /device:TPU:0, one launch (start us, length us, event | category | flops | bytes accessed | tf_op | source)
XLA Modules:
  0.0 1013.9 jit_solution(5791942358656270327)
XLA Ops:
  9.5 3.1 collective-permute-start
  13.3 31.6 %collective-permute-done = bf16[192,2304]{1,0:T(8,128)(2,1)S(1)} collective-permute-done((bf16[192,2304]{1,0:T(8,128)(2,1)S(1)}, bf16[192,2304]{1,0:T(8,128)(2,1)S(1)}, u32[]{:S(2)}, u32[]{:S(2)}) %collective-permute-start) | collective-permute-done | bytes 884768 | tf_op jit(solution)/shard_map/ppermute | solution.py:31
  44.9 6.3 collective-permute-start.1
  51.2 53.3 %all_gather.86 = bf16[768,128]{1,0:T(8,128)(2,1)S(1)} all-gather(bf16[192,128]{1,0:T(8,128)(2,1)S(1)} %copy-done.183), channel_id=1, replica_groups=mesh['rep'=8,'shard'=4] {'shard'}, dimensions={0}, use_global_device_ids=true | all-gather | bytes 245760 | tf_op jit(solution)/shard_map/all_gather | solution.py:177
  112.1 58.7 %all-reduce.15 = (bf16[768]{0:T(1024)(128)(2,1)S(1)}, bf16[768]{0:T(1024)(128)(2,1)S(1)}, bf16[768]{0:T(1024)(128)(2,1)}, bf16[768]{0:T(1024)(128)(2,1)}) all-reduce(bf16[768]{0:T(1024)(128)(2,1)S(1)} %dynamic-update-slice.1, bf16[768]{0:T(1024)(128)(2,1)S(1)} %dynamic-update-slice, ...), channel_id=1, replica_groups=mesh['rep'=8,'shard'=4] {'shard'}, use_global_device_ids=true, to_apply=%add.5 | all-reduce | flops 3072 | bytes 12288
  182.5 3.5 convolution_convert_fusion
  208.5 3.2 convolution_convert_fusion.1
  270.3 24.4 %all-gather.2 = bf16[48,128,64]{1,2,0:T(8,128)(2,1)} all-gather(bf16[12,128,64]{1,2,0:T(8,128)(2,1)S(1)} %convolution_convert_fusion.6), channel_id=4, replica_groups=mesh['rep'=8,'shard'=4] {'shard'}, dimensions={0}, use_global_device_ids=true | all-gather | bytes 983040 | tf_op jit(solution)/shard_map/all_gather | solution.py:41
  294.8 13.4 %all-gather.9 = bf16[4,12,128]{2,1,0:T(8,128)(2,1)S(1)} all-gather(bf16[1,12,128]{2,1,0:T(8,128)(2,1)S(1)} %bitcast.581), channel_id=5, replica_groups=mesh['rep'=8,'shard'=4] {'shard'}, dimensions={0}, use_global_device_ids=true | all-gather | bytes 15360 | tf_op jit(solution)/shard_map/all_gather | solution.py:41
  308.1 6.6 while.63
  330.5 4.5 fusion.40
  358.4 16.4 %all-gather = bf16[48,128,64]{1,2,0:T(8,128)(2,1)} all-gather(bf16[12,128,64]{1,2,0:T(8,128)(2,1)S(1)} %convolution_convert_fusion.7), channel_id=2, replica_groups=mesh['rep'=8,'shard'=4] {'shard'}, dimensions={0}, use_global_device_ids=true | all-gather | bytes 983040 | tf_op jit(solution)/shard_map/all_gather | solution.py:41
  374.8 13.3 %all-gather.8 = bf16[4,12,128]{2,1,0:T(8,128)(2,1)S(1)} all-gather(bf16[1,12,128]{2,1,0:T(8,128)(2,1)S(1)} %bitcast.580), channel_id=3, replica_groups=mesh['rep'=8,'shard'=4] {'shard'}, dimensions={0}, use_global_device_ids=true | all-gather | bytes 15360 | tf_op jit(solution)/shard_map/all_gather | solution.py:41
  388.1 6.6 while.62
  412.2 4.3 fusion.42
  422.4 5.6 fusion.215
  428.0 3.2 fusion.214
  431.2 6.2 fusion.21
  438.6 3.9 fusion.265
  442.6 3.4 fusion.14
  455.5 4.4 fusion.255
  462.4 4.0 fusion.29
  470.8 3.7 fusion.254
  477.2 16.5 %all-gather.6 = bf16[48,128,64]{1,2,0:T(8,128)(2,1)} all-gather(bf16[12,128,64]{1,2,0:T(8,128)(2,1)S(1)} %copy-done.153), channel_id=8, replica_groups=mesh['rep'=8,'shard'=4] {'shard'}, dimensions={0}, use_global_device_ids=true | all-gather | bytes 983040 | tf_op jit(solution)/shard_map/all_gather | solution.py:66
  493.7 13.4 %all-gather.11 = bf16[4,12,128]{2,1,0:T(8,128)(2,1)S(1)} all-gather(bf16[1,12,128]{2,1,0:T(8,128)(2,1)S(1)} %bitcast.583), channel_id=9, replica_groups=mesh['rep'=8,'shard'=4] {'shard'}, dimensions={0}, use_global_device_ids=true | all-gather | bytes 15360 | tf_op jit(solution)/shard_map/all_gather | solution.py:66
  507.2 4.3 while.61
  518.9 3.1 copy.227
  539.1 16.4 %all-gather.4 = bf16[48,128,64]{1,2,0:T(8,128)(2,1)} all-gather(bf16[12,128,64]{1,2,0:T(8,128)(2,1)S(1)} %get-tuple-element.652), channel_id=6, replica_groups=mesh['rep'=8,'shard'=4] {'shard'}, dimensions={0}, use_global_device_ids=true | all-gather | bytes 983040 | tf_op jit(solution)/shard_map/all_gather | solution.py:66
  555.5 13.1 %all-gather.10 = bf16[4,12,128]{2,1,0:T(8,128)(2,1)S(1)} all-gather(bf16[1,12,128]{2,1,0:T(8,128)(2,1)S(1)} %bitcast.582), channel_id=7, replica_groups=mesh['rep'=8,'shard'=4] {'shard'}, dimensions={0}, use_global_device_ids=true | all-gather | bytes 15360 | tf_op jit(solution)/shard_map/all_gather | solution.py:66
  568.7 4.5 while.60
  580.6 3.2 copy.205
  620.5 5.4 add_bitcast_fusion
  625.9 3.8 add_bitcast_fusion.2
  638.0 3.6 copy.208
  653.7 3.2 add_convert_fusion.2
  658.1 3.1 fusion.213
  661.2 3.8 add_convert_fusion.1
  666.2 4.2 fusion.129
  670.5 3.9 add_convert_fusion
  681.7 3.5 fusion.119
  689.7 5.2 fusion.78
  695.0 29.2 %reduce-scatter.6.cloned.1.call-done = bf16[192,2304]{1,0:T(8,128)(2,1)} async-done(((bf16[768,2304]{1,0:T(8,128)(2,1)}), bf16[192,2304]{1,0:T(8,128)(2,1)}) %reduce-scatter.6.cloned.1.call-update) | async-done | bytes 884752 | tf_op jit(solution)/shard_map/reduce_scatter | solution.py:322
  724.2 87.9 %reduce-scatter.12.cloned.1.call-done = bf16[192,3072]{1,0:T(8,128)(2,1)} async-done(((bf16[768,3072]{1,0:T(8,128)(2,1)}), bf16[192,3072]{1,0:T(8,128)(2,1)}) %reduce-scatter.12.cloned.1.call-update) | async-done | bytes 1179664 | tf_op jit(solution)/shard_map/reduce_scatter | solution.py:337
  812.1 88.1 %reduce-scatter.14.cloned.1.call-done = bf16[768,768]{1,0:T(8,128)(2,1)} async-done(((bf16[3072,768]{1,0:T(8,128)(2,1)}), bf16[768,768]{1,0:T(8,128)(2,1)}) %reduce-scatter.14.cloned.1.call-update) | async-done | bytes 1179664 | tf_op jit(solution)/shard_map/reduce_scatter | solution.py:340
  900.9 11.1 %all-reduce.14 = (bf16[768]{0:T(1024)(128)(2,1)S(1)}, bf16[768]{0:T(1024)(128)(2,1)S(1)}, bf16[768]{0:T(1024)(128)(2,1)S(1)}, bf16[768]{0:T(1024)(128)(2,1)S(1)}) all-reduce(bf16[768]{0:T(1024)(128)(2,1)S(1)} %copy-done.231, bf16[768]{0:T(1024)(128)(2,1)S(1)} %add_convert_fusion.14, ...), channel_id=10, replica_groups=mesh['rep'=8,'shard'=4] {'shard'}, use_global_device_ids=true, to_apply=%region_70.71.clone | all-reduce | flops 3072 | bytes 12288
  912.3 5.4 fusion.79
  923.0 24.6 %all-reduce.12 = (bf16[192]{0:T(256)(128)(2,1)S(1)}, bf16[192]{0:T(256)(128)(2,1)S(1)}, bf16[192,128]{1,0:T(8,128)(2,1)S(1)}, bf16[192]{0:T(256)(128)(2,1)S(1)}, bf16[192]{0:T(256)(128)(2,1)S(1)}) all-reduce(bf16[192]{0:T(256)(128)(2,1)S(1)} %dynamic-slice.5, ...), channel_id=1, replica_groups=mesh['rep'=8,'shard'=4] {'rep'}, use_global_device_ids=true, to_apply=%region_71.72 | all-reduce | flops 25344 | bytes 101376 | tf_op jit(solution)/shard_map/psum | solution.py:345
  950.5 49.7 %all-reduce.18.cloned.1.call-done = (bf16[192,2304]{1,0:T(8,128)(2,1)}, bf16[192,768]{1,0:T(8,128)(2,1)}, bf16[192,3072]{1,0:T(8,128)(2,1)}, bf16[768,768]{1,0:T(8,128)(2,1)}) async-done(((bf16[192,2304]{1,0:T(8,128)(2,1)}, bf16[192,768]{1,0:T(8,128)(2,1)}, bf16[192,3072]{1,0:T(8,128)(2,1)}, bf16[768,768]{1,0:T(8,128)(2,1)}), (bf16[192,2304]{1,0:T(8,128)(2,1)}, bf16[192,768]{1,0:T(8,128)(2,1)}, ...) | async-done | bytes 3538960 | tf_op jit(solution)/shard_map/psum | solution.py:347
  (829 shorter events, 322.8 us)
Async XLA Ops:
  7.2 328.9 %all-gather.17.cloned.1.call-start = ((), (), s32[]{:S(2)}) async-start(), calls=%async_computation.5 | async-start | bytes 1474560 | tf_op jit(solution)/shard_map/all_gather | solution.py:178
  7.9 414.4 %all-gather.19.cloned.1.call-start = ((), (), s32[]{:S(2)}) async-start(), calls=%async_computation.6 | async-start | bytes 5898240 | tf_op jit(solution)/shard_map/all_gather | solution.py:181
  8.7 42.5 %copy-start.183 = (bf16[192,128]{1,0:T(8,128)(2,1)S(1)}, bf16[192,128]{1,0:T(8,128)(2,1)}, u32[]{:S(2)}) copy-start(bf16[192,128]{1,0:T(8,128)(2,1)} %param.23) | copy-start | bytes 147460
  8.7 422.5 %all-gather.21.cloned.1.call-start = ((), (), s32[]{:S(2)}) async-start(), calls=%async_computation.7 | async-start | bytes 5898240 | tf_op jit(solution)/shard_map/all_gather | solution.py:182
  9.4 672.3 %all-gather.23.cloned.1.call-start = ((), (), s32[]{:S(2)}) async-start(), calls=%async_computation.8 | async-start | bytes 4423680 | tf_op jit(solution)/shard_map/all_gather | solution.py:243
  9.5 35.4 %collective-permute-start = (bf16[192,2304]{1,0:T(8,128)(2,1)S(1)}, bf16[192,2304]{1,0:T(8,128)(2,1)S(1)}, u32[]{:S(2)}, u32[]{:S(2)}) collective-permute-start(bf16[192,2304]{1,0:T(8,128)(2,1)S(1)} %copy-done.84), channel_id=1, source_target_pairs={{0,1},{1,2},{2,3},{3,0},{4,5},{5,6},{6,7},{7,4},{8,9},{9,10},{10,1... | collective-permute-start | bytes 2654216 | tf_op jit(solution)/shard_map/ppermute | solution.py:31
  12.6 682.4 %reduce-scatter.10.cloned.1.call-start = ((), (), s32[]{:S(2)}) async-start(), calls=%async_computation.11 | async-start | bytes 1474560 | tf_op jit(solution)/shard_map/reduce_scatter | solution.py:328
  12.9 91.8 %copy-start.184 = (f32[256]{0:T(256)}, f32[256]{0:T(256)S(1)}, u32[]{:S(2)}) copy-start(f32[256]{0:T(256)S(1)} %get-tuple-element.658) | copy-start | bytes 3076
  12.9 91.8 %copy-start.193 = (f32[256]{0:T(256)}, f32[256]{0:T(256)S(1)}, u32[]{:S(2)}) copy-start(f32[256]{0:T(256)S(1)} %get-tuple-element.657) | copy-start | bytes 3076
  13.2 91.4 %copy-start.221 = (f32[256]{0:T(256)}, f32[256]{0:T(256)S(1)}, u32[]{:S(2)}) copy-start(f32[256]{0:T(256)S(1)} %get-tuple-element.512) | copy-start | bytes 3076
  13.2 96.0 %copy-start.223 = (f32[256]{0:T(256)}, f32[256]{0:T(256)S(1)}, u32[]{:S(2)}) copy-start(f32[256]{0:T(256)S(1)} %get-tuple-element.511) | copy-start | bytes 3076
  44.9 61.4 %copy-start.136 = (bf16[192,2304]{1,0:T(8,128)(2,1)}, bf16[192,2304]{1,0:T(8,128)(2,1)S(1)}, u32[]{:S(2)}) copy-start(bf16[192,2304]{1,0:T(8,128)(2,1)S(1)} %collective-permute-done) | copy-start | bytes 2654212
  44.9 64.3 %collective-permute-start.1 = (bf16[192,2304]{1,0:T(8,128)(2,1)S(1)}, bf16[192,2304]{1,0:T(8,128)(2,1)}, u32[]{:S(2)}, u32[]{:S(2)}) collective-permute-start(bf16[192,2304]{1,0:T(8,128)(2,1)S(1)} %collective-permute-done), channel_id=1, source_target_pairs={{0,1},{1,2},{2,3},{3,0},{4,5},{5,6},{6,7},{7,4},{8,9},{9,10},{10,1... | collective-permute-start | bytes 2654216 | tf_op jit(solution)/shard_map/ppermute | solution.py:31
  109.2 71.0 %collective-permute-start.2 = (bf16[192,2304]{1,0:T(8,128)(2,1)}, bf16[192,2304]{1,0:T(8,128)(2,1)}, u32[]{:S(2)}, u32[]{:S(2)}) collective-permute-start(bf16[192,2304]{1,0:T(8,128)(2,1)} %collective-permute-done.1), channel_id=1, source_target_pairs={{0,1},{1,2},{2,3},{3,0},{4,5},{5,6},{6,7},{7,4},{8,9},{9,10},{10,1... | collective-permute-start | bytes 2654216 | tf_op jit(solution)/shard_map/ppermute | solution.py:31
  172.3 17.5 %copy-start.77 = (bf16[12,64,1,64]{1,3,0,2:T(8,128)(2,1)}, bf16[12,64,1,64]{1,3,0,2:T(8,128)(2,1)S(1)}, u32[]{:S(2)}) copy-start(bf16[12,64,1,64]{1,3,0,2:T(8,128)(2,1)S(1)} %copy.272) | copy-start | bytes 294916
  172.6 24.2 %copy-start.79 = (bf16[12,64,1,64]{1,3,0,2:T(8,128)(2,1)}, bf16[12,64,1,64]{1,3,0,2:T(8,128)(2,1)S(1)}, u32[]{:S(2)}) copy-start(bf16[12,64,1,64]{1,3,0,2:T(8,128)(2,1)S(1)} %copy.273) | copy-start | bytes 294916
  191.7 62.3 %copy-start.18 = (f32[256,12,64]{0,2,1:T(8,128)}, f32[256,12,64]{0,2,1:T(8,128)S(1)}, u32[]{:S(2)}) copy-start(f32[256,12,64]{0,2,1:T(8,128)S(1)} %get-tuple-element.626) | copy-start | bytes 2359300
  200.8 69.1 %copy-start.68 = (bf16[256,12,64]{0,2,1:T(8,128)(2,1)}, bf16[256,12,64]{0,2,1:T(8,128)(2,1)S(1)}, u32[]{:S(2)}) copy-start(bf16[256,12,64]{0,2,1:T(8,128)(2,1)S(1)} %divide_convert_fusion) | copy-start | bytes 1179652
  268.7 26.0 %copy-start.86 = (bf16[256,768]{0,1:T(8,128)(2,1)}, bf16[256,768]{0,1:T(8,128)(2,1)S(1)}, u32[]{:S(2)}) copy-start(bf16[256,768]{0,1:T(8,128)(2,1)S(1)} %copy.174) | copy-start | bytes 1179652
  269.9 24.8 %copy-start.206 = (bf16[12,128]{1,0:T(8,128)(2,1)S(1)}, bf16[12,128]{1,0:T(8,128)(2,1)}, u32[]{:S(2)}) copy-start(bf16[12,128]{1,0:T(8,128)(2,1)} %fusion.139) | copy-start | bytes 9220
  329.0 6.0 copy-start.141
  356.8 18.1 %copy-start.88 = (bf16[256,768]{0,1:T(8,128)(2,1)}, bf16[256,768]{0,1:T(8,128)(2,1)S(1)}, u32[]{:S(2)}) copy-start(bf16[256,768]{0,1:T(8,128)(2,1)S(1)} %copy.157) | copy-start | bytes 1179652
  358.0 16.8 %copy-start.205 = (bf16[12,128]{1,0:T(8,128)(2,1)S(1)}, bf16[12,128]{1,0:T(8,128)(2,1)}, u32[]{:S(2)}) copy-start(bf16[12,128]{1,0:T(8,128)(2,1)} %fusion.140) | copy-start | bytes 9220
  422.4 5.7 copy-start.29
  422.4 5.6 copy-start.198
  422.4 5.6 copy-start.210
  422.4 5.6 copy-start.242
  431.2 11.3 %copy-start.241 = (bf16[3072,768]{1,0:T(8,128)(2,1)S(1)}, bf16[3072,768]{1,0:T(8,128)(2,1)}, u32[]{:S(2)}) copy-start(bf16[3072,768]{1,0:T(8,128)(2,1)} %all-gather.21.cloned.1.call-done) | copy-start | bytes 14155780
  438.6 7.4 slice-start.2
  620.4 5.4 copy-start.59
  620.4 5.4 copy-start.63
  620.5 5.4 copy-start.122
  620.5 5.4 copy-start.192
  629.8 94.5 %reduce-scatter.6.cloned.1.call-start = ((), (), s32[]{:S(2)}) async-start(), calls=%async_computation.9 | async-start | bytes 4423680 | tf_op jit(solution)/shard_map/reduce_scatter | solution.py:322
  641.6 5.9 copy-start.17
  641.6 5.9 copy-start.145
  657.0 155.1 %reduce-scatter.12.cloned.1.call-start = ((), (), s32[]{:S(2)}) async-start(), calls=%async_computation.12 | async-start | bytes 5898240 | tf_op jit(solution)/shard_map/reduce_scatter | solution.py:337
  665.1 235.1 %reduce-scatter.14.cloned.1.call-start = ((), (), s32[]{:S(2)}) async-start(), calls=%async_computation.13 | async-start | bytes 5898240 | tf_op jit(solution)/shard_map/reduce_scatter | solution.py:340
  674.4 248.6 %reduce-scatter.8.cloned.1.call-start = ((), (), s32[]{:S(2)}) async-start(), calls=%async_computation.10 | async-start | bytes 245760 | tf_op jit(solution)/shard_map/reduce_scatter | solution.py:325
  689.3 310.8 %all-reduce.18.cloned.1.call-start = ((), (), s32[]{:S(2)}) async-start(), calls=%async_computation.14 | async-start | bytes 7077888 | tf_op jit(solution)/shard_map/psum | solution.py:347
  689.6 5.3 copy-start.238
  689.7 5.3 copy-start.239
  689.7 5.3 copy-start.236
  689.7 5.3 copy-start.237
  912.3 6.4 copy-start.233
  912.3 6.4 copy-start.232
  912.3 6.4 copy-start.110
  912.3 6.4 copy-start.112
  (217 other events, 558.3 us)
Sparse Core Ops, SparseCore 0:
  9.6 43.9 all-gather.16
  55.2 117.4 all-gather.18
  174.2 90.6 all-gather.20
  266.3 75.3 all-gather.22
  629.9 27.0 reduce-scatter.9
  659.1 65.0 reduce-scatter.5
  726.5 85.5 reduce-scatter.11
  814.4 85.7 reduce-scatter.13
  903.0 19.8 reduce-scatter.7
  926.9 73.1 all-reduce.17
